TPU v7x, 32 devices: a whole 2x2x4 slice. The times are simulated.
32 devices in a mesh: item: 8 (over z, y), code: 4 (over x, core).
Axes of the slice: x: 2, y: 2, z: 4, core: 2. Of those that a mesh axis runs over, the one named last changes fastest.
Arguments:
- residuals: float32 [256, 32768], P('code', 'item'), may hold values from -6 to 6
- codebook: float32 [256, 32768], P('item', 'code'), may hold values from -6 to 6
- item_weight: float32 [32768], P('item'), may hold values from 1 to 100
- code_capacity: float32 [32768], P('code'), may hold values from 0.25 to 4
- pairs: int32 [512, 64], P('item', 'code'), may hold values from -1 to 127, as said below
Outputs:
- item_potential: float32 [32768], P('item')
- code_potential: float32 [32768], P('code')
Inputs may be any that keep to these rules, and one draw needn't show every extreme that they name: `pairs`: each entry is -1 (no candidate) or a code block's number within the code shard of its slot column. Within one item block and one code shard the live entries are distinct, the first slot is always live, and between 1 and 8 are live; some device holds exactly 8 live slots in every item block. Every code block is named by some item block.
All inputs are finite; a program needn't handle non-finite values.
Results may differ from a plain program's by a relative error of at most 0.0003.
Values sent between devices are 32-bit elements; how exact they have to be, the bound alone decides.
No kernel may reach another device: no remote copies, remote signals or barrier semaphores. Data moves between devices by JAX's collectives and lax.ppermute only.
A program may use at most 128 MiB of HBM per device.

v0:
```python
import math
import jax
import jax.numpy as jnp
from jax import lax
from jax.sharding import PartitionSpec as P

BLOCK = 64
ITERS = 3
masked_score = -1e30
softness_factor = 0.1


def body(residuals, codebook, item_weight, code_capacity, pairs):
    item_columns = lax.all_gather(residuals, "code", axis=0, tiled=True)
    code_cols = lax.all_gather(codebook, "item", axis=0, tiled=True)
    embedding_width = item_columns.shape[0]
    item_count = item_columns.shape[1]
    code_count = code_cols.shape[1]
    item_blocks = item_count // BLOCK
    code_blocks = code_count // BLOCK
    logit_scale = 1.0 / (softness_factor * math.sqrt(embedding_width))
    weight_sum = lax.psum(jnp.sum(item_weight), "item")
    capacity_sum = lax.psum(jnp.sum(code_capacity), "code")
    item_logmass = jnp.log(item_weight) - jnp.log(weight_sum)
    code_logmass = jnp.log(code_capacity) - jnp.log(capacity_sum)
    slot_order = jnp.argsort((pairs < 0).astype(jnp.int32), axis=1, stable=True)[
        :, : pairs.shape[1] // 2
    ]
    chosen = jnp.take_along_axis(pairs, slot_order, axis=1)
    is_live = chosen >= 0
    safe_ids = jnp.where(is_live, chosen, 0)
    target = jnp.where(is_live, chosen, code_blocks)
    item_split_cols = item_columns.reshape(embedding_width, item_blocks, BLOCK)
    code_column_splits = code_cols.reshape(embedding_width, code_blocks, BLOCK)
    group = math.gcd(item_blocks, 8)
    group_count = item_blocks // group

    def build_tiles(own, ids, live):
        picked = code_column_splits[:, ids, :]
        scores = (
            jnp.einsum("rbi,rbsj->bsij", own, picked, precision=lax.Precision.HIGHEST) * logit_scale
        )
        return jnp.where(live[:, :, None, None], scores, masked_score)

    reduce_fn = lambda tiles, ids, portion: tiles

    def one_group(group_index):
        start = group_index * group
        own = lax.dynamic_slice_in_dim(item_split_cols, start, group, 1)
        ids = lax.dynamic_slice_in_dim(safe_ids, start, group, 0)
        live = lax.dynamic_slice_in_dim(is_live, start, group, 0)
        portion = lax.dynamic_slice_in_dim(safe_ids, start, group, 0)
        return reduce_fn(build_tiles(own, ids, live), ids, portion)

    results = lax.map(one_group, jnp.arange(group_count, dtype=jnp.int32))
    saved_tile_blocks = results.reshape((item_blocks,) + results.shape[2:])

    def run_pass(reduce_fn, extra):
        return reduce_fn(saved_tile_blocks, safe_ids, extra)

    flat_target = target.reshape(-1)
    flat_rows = flat_target.shape[0]
    row_group = math.gcd(flat_rows, 256)
    one_hot = flat_target[:, None] == jnp.arange(code_blocks, dtype=jnp.int32)[None, :]
    one_hot_groups = one_hot.reshape(flat_rows // row_group, row_group, code_blocks)
    one_hot_float = one_hot.astype(jnp.float32)
    code_potential = jnp.zeros((code_count,), jnp.float32)
    item_potential = jnp.zeros((item_count,), jnp.float32)
    for sweep in range(ITERS):
        code_split = code_potential.reshape(code_blocks, BLOCK)

        def row_reduce(tiles, ids, portion):
            logits = tiles + code_split[ids][:, :, None, :]
            block_peak = jnp.max(logits, axis=(1, 3))
            block_total = jnp.sum(jnp.exp(logits - block_peak[:, None, :, None]), axis=(1, 3))
            return (block_peak, block_total)

        row_peak, row_total = run_pass(row_reduce, safe_ids)
        row_peak = row_peak.reshape(item_count)
        row_total = row_total.reshape(item_count)
        merged_peak = lax.pmax(row_peak, "code")
        merged_total = lax.psum(row_total * jnp.exp(row_peak - merged_peak), "code")
        item_potential = item_logmass - (merged_peak + jnp.log(merged_total))
        item_split = item_potential.reshape(item_blocks, BLOCK)

        def col_reduce(tiles, ids, portion):
            logits = tiles + portion[:, None, :, None]
            block_peak = jnp.max(logits, axis=2)
            block_total = jnp.sum(jnp.exp(logits - block_peak[:, :, None, :]), axis=2)
            return (block_peak, block_total)

        tile_peak, tile_total = run_pass(col_reduce, item_split)
        peak_flat = tile_peak.reshape(flat_rows, BLOCK)
        total_flat = tile_total.reshape(flat_rows, BLOCK)
        peak_groups = peak_flat.reshape(flat_rows // row_group, row_group, BLOCK)

        def peak_step(carry, pieces):
            hot, peaks = pieces
            candidate = jnp.max(jnp.where(hot[:, :, None], peaks[:, None, :], masked_score), axis=0)
            return (jnp.maximum(carry, candidate), None)

        col_peak, unused = lax.scan(
            peak_step,
            jnp.full((code_blocks, BLOCK), masked_score, jnp.float32),
            (one_hot_groups, peak_groups),
        )
        padded_peak = jnp.concatenate(
            [col_peak, jnp.full((1, BLOCK), masked_score, jnp.float32)], axis=0
        )
        spread = total_flat * jnp.exp(peak_flat - padded_peak[flat_target])
        col_total = jnp.dot(
            one_hot_float.T,
            spread,
            precision=lax.Precision.HIGHEST,
            preferred_element_type=jnp.float32,
        )
        col_peak = col_peak.reshape(code_count)
        col_total = col_total.reshape(code_count)
        joined_peak = lax.pmax(col_peak, "item")
        joined_total = lax.psum(col_total * jnp.exp(col_peak - joined_peak), "item")
        code_potential = code_logmass - (joined_peak + jnp.log(joined_total))
    return (item_potential, code_potential)


def solution(mesh):
    placed = (P("code", "item"), P("item", "code"), P("item"), P("code"), P("item", "code"))
    return jax.shard_map(
        body, mesh=mesh, in_specs=placed, out_specs=(P("item"), P("code")), check_vma=False
    )
```

profile of v0, /device:TPU:0, one launch (start us, length us, event | category | flops | bytes accessed | tf_op | source)
XLA Modules:
  0.0 706.6 jit_solution(5821192888771860012)
XLA Ops:
  8.7 1.3 reduce_sum.72
  10.0 23.8 %psum.56 = f32[]{:T(128)} all-reduce(f32[]{:T(128)} %reduce_sum.72), channel_id=1, replica_groups=mesh['item'=8,'code'=4] {'item'}, use_global_device_ids=true, to_apply=%region_1.0 | all-reduce | flops 1 | bytes 8 | tf_op jit(solution)/shard_map/psum | solution.py:22
  35.4 3.9 gather_fusion.7
  41.4 1.0 gather_fusion.1
  42.6 4.1 all-gather.5.cloned.1.call-done
  46.8 5.6 copy.38
  52.4 121.0 %all-gather.3.cloned.1.call-done = f32[256,8192]{1,0:T(8,128)} async-done(((f32[32,8192]{1,0:T(8,128)}), f32[256,8192]{1,0:T(8,128)}) %all-gather.3.cloned.1.call-update) | async-done | bytes 8388624 | tf_op jit(solution)/shard_map/all_gather | solution.py:15
  173.4 9.0 %copy.37 = f32[256,8192]{0,1:T(8,128)} copy(f32[256,8192]{1,0:T(8,128)} %all-gather.3.cloned.1.call-done) | data formatting | bytes 16777216 | tf_op jit(solution)/shard_map/all_gather | solution.py:15
  182.4 120.6 %while.43 = (s32[]{:T(128)}, f32[8,8,8,64,64]{3,4,2,1,0:T(8,128)}, s32[8]{0:T(128)S(1)}, pred[64,8]{0,1:T(8,128)(4,1)S(1)}, s32[64,8]{0,1:T(8,128)S(1)}, /*index...) while((s32[]{:T(128)}, f32[8,8,8,64,64]{3,4,2,1,0:T(8,128)}, ...), condition=%wide.region_4.0_spmd, body=%wide.region_3.0_spmd.sunk | while | flops 805831872 | bytes 15212019 | solution.py:55
  183.9 6.2 gather_fusion
  190.2 7.3 %bitcast_dynamic-update-slice_fusion.2 = f32[8,8,8,64,64]{3,4,2,1,0:T(8,128)} fusion(f32[8,8,8,64,64]{3,4,2,1,0:T(8,128)} %get-tuple-element.349, s32[]{:T(128)} %get-tuple-element.348, f32[256,8,8,64]{0,3,2,1:T(8,128)} %bitcast.88, pred[8,8]{1,0:T(8,128)(4,1)S(1)} %copy.63, f32[256,64,64]{0,2,1:T(8,128)} %get-tuple-element.365, s32[]{:T(128)S(6)} %select_n.148), kind=kOutput, calls=%fused_computation.8.clone.1 | convolution fusion | flops 805830656 | bytes 6816324 | tf_op jit(solution)/shard_map/while/body/eval_jaxpr/rbi,rbsj->bsij/dot_general | solution.py:41
  199.0 6.2 gather_fusion
  205.3 7.2 %bitcast_dynamic-update-slice_fusion.2 = f32[8,8,8,64,64]{3,4,2,1,0:T(8,128)} fusion(f32[8,8,8,64,64]{3,4,2,1,0:T(8,128)} %get-tuple-element.349, s32[]{:T(128)} %get-tuple-element.348, f32[256,8,8,64]{0,3,2,1:T(8,128)} %bitcast.88, pred[8,8]{1,0:T(8,128)(4,1)S(1)} %copy.63, f32[256,64,64]{0,2,1:T(8,128)} %get-tuple-element.365, s32[]{:T(128)S(6)} %select_n.148), kind=kOutput, calls=%fused_computation.8.clone.1 | convolution fusion | flops 805830656 | bytes 6816324 | tf_op jit(solution)/shard_map/while/body/eval_jaxpr/rbi,rbsj->bsij/dot_general | solution.py:41
  214.0 6.2 gather_fusion
  220.3 7.3 %bitcast_dynamic-update-slice_fusion.2 = f32[8,8,8,64,64]{3,4,2,1,0:T(8,128)} fusion(f32[8,8,8,64,64]{3,4,2,1,0:T(8,128)} %get-tuple-element.349, s32[]{:T(128)} %get-tuple-element.348, f32[256,8,8,64]{0,3,2,1:T(8,128)} %bitcast.88, pred[8,8]{1,0:T(8,128)(4,1)S(1)} %copy.63, f32[256,64,64]{0,2,1:T(8,128)} %get-tuple-element.365, s32[]{:T(128)S(6)} %select_n.148), kind=kOutput, calls=%fused_computation.8.clone.1 | convolution fusion | flops 805830656 | bytes 6816324 | tf_op jit(solution)/shard_map/while/body/eval_jaxpr/rbi,rbsj->bsij/dot_general | solution.py:41
  229.0 6.2 gather_fusion
  235.4 7.3 %bitcast_dynamic-update-slice_fusion.2 = f32[8,8,8,64,64]{3,4,2,1,0:T(8,128)} fusion(f32[8,8,8,64,64]{3,4,2,1,0:T(8,128)} %get-tuple-element.349, s32[]{:T(128)} %get-tuple-element.348, f32[256,8,8,64]{0,3,2,1:T(8,128)} %bitcast.88, pred[8,8]{1,0:T(8,128)(4,1)S(1)} %copy.63, f32[256,64,64]{0,2,1:T(8,128)} %get-tuple-element.365, s32[]{:T(128)S(6)} %select_n.148), kind=kOutput, calls=%fused_computation.8.clone.1 | convolution fusion | flops 805830656 | bytes 6816324 | tf_op jit(solution)/shard_map/while/body/eval_jaxpr/rbi,rbsj->bsij/dot_general | solution.py:41
  244.1 6.2 gather_fusion
  250.4 7.3 %bitcast_dynamic-update-slice_fusion.2 = f32[8,8,8,64,64]{3,4,2,1,0:T(8,128)} fusion(f32[8,8,8,64,64]{3,4,2,1,0:T(8,128)} %get-tuple-element.349, s32[]{:T(128)} %get-tuple-element.348, f32[256,8,8,64]{0,3,2,1:T(8,128)} %bitcast.88, pred[8,8]{1,0:T(8,128)(4,1)S(1)} %copy.63, f32[256,64,64]{0,2,1:T(8,128)} %get-tuple-element.365, s32[]{:T(128)S(6)} %select_n.148), kind=kOutput, calls=%fused_computation.8.clone.1 | convolution fusion | flops 805830656 | bytes 6816324 | tf_op jit(solution)/shard_map/while/body/eval_jaxpr/rbi,rbsj->bsij/dot_general | solution.py:41
  259.2 6.2 gather_fusion
  265.6 7.2 %bitcast_dynamic-update-slice_fusion.2 = f32[8,8,8,64,64]{3,4,2,1,0:T(8,128)} fusion(f32[8,8,8,64,64]{3,4,2,1,0:T(8,128)} %get-tuple-element.349, s32[]{:T(128)} %get-tuple-element.348, f32[256,8,8,64]{0,3,2,1:T(8,128)} %bitcast.88, pred[8,8]{1,0:T(8,128)(4,1)S(1)} %copy.63, f32[256,64,64]{0,2,1:T(8,128)} %get-tuple-element.365, s32[]{:T(128)S(6)} %select_n.148), kind=kOutput, calls=%fused_computation.8.clone.1 | convolution fusion | flops 805830656 | bytes 6816324 | tf_op jit(solution)/shard_map/while/body/eval_jaxpr/rbi,rbsj->bsij/dot_general | solution.py:41
  274.3 6.2 gather_fusion
  280.6 7.3 %bitcast_dynamic-update-slice_fusion.2 = f32[8,8,8,64,64]{3,4,2,1,0:T(8,128)} fusion(f32[8,8,8,64,64]{3,4,2,1,0:T(8,128)} %get-tuple-element.349, s32[]{:T(128)} %get-tuple-element.348, f32[256,8,8,64]{0,3,2,1:T(8,128)} %bitcast.88, pred[8,8]{1,0:T(8,128)(4,1)S(1)} %copy.63, f32[256,64,64]{0,2,1:T(8,128)} %get-tuple-element.365, s32[]{:T(128)S(6)} %select_n.148), kind=kOutput, calls=%fused_computation.8.clone.1 | convolution fusion | flops 805830656 | bytes 6816324 | tf_op jit(solution)/shard_map/while/body/eval_jaxpr/rbi,rbsj->bsij/dot_general | solution.py:41
  289.4 6.2 gather_fusion
  295.7 7.3 %bitcast_dynamic-update-slice_fusion.2 = f32[8,8,8,64,64]{3,4,2,1,0:T(8,128)} fusion(f32[8,8,8,64,64]{3,4,2,1,0:T(8,128)} %get-tuple-element.349, s32[]{:T(128)} %get-tuple-element.348, f32[256,8,8,64]{0,3,2,1:T(8,128)} %bitcast.88, pred[8,8]{1,0:T(8,128)(4,1)S(1)} %copy.63, f32[256,64,64]{0,2,1:T(8,128)} %get-tuple-element.365, s32[]{:T(128)S(6)} %select_n.148), kind=kOutput, calls=%fused_computation.8.clone.1 | convolution fusion | flops 805830656 | bytes 6816324 | tf_op jit(solution)/shard_map/while/body/eval_jaxpr/rbi,rbsj->bsij/dot_general | solution.py:41
  302.9 9.4 %add_reduce_fusion.5 = f32[8,8,64]{2,1,0:T(8,128)S(1)} fusion(f32[8,8,8,64,64]{3,4,2,1,0:T(8,128)} %get-tuple-element.107, f32[8,8,8,64]{3,2,1,0:T(8,128)S(1)} %bitcast.97), kind=kLoop, calls=%fused_computation.39 | loop fusion | flops 4190208 | bytes 8536064 | tf_op jit(solution)/shard_map/reduce_max | solution.py:74
  312.3 1.3 copy-done.1
  313.7 5.1 exponential_reduce_fusion.5
  319.0 10.2 %pmax.42 = f32[4096]{0:T(1024)S(1)} all-reduce(f32[4096]{0:T(1024)S(1)} %reshape.247), channel_id=1, replica_groups=mesh['item'=8,'code'=4] {'code'}, use_global_device_ids=true, to_apply=%region_8.9 | all-reduce | flops 4096 | bytes 32768 | tf_op jit(solution)/shard_map/pmax | solution.py:81
  329.2 11.4 %all-reduce.3 = (f32[4096]{0:T(1024)S(1)}, f32[]{:T(128)}) all-reduce(f32[4096]{0:T(1024)S(1)} %exponential_multiply_fusion.5, f32[]{:T(128)} %reduce_sum.73), channel_id=1, replica_groups=mesh['item'=8,'code'=4] {'code'}, use_global_device_ids=true, to_apply=%region_10.11 | all-reduce | flops 4097 | bytes 32776 | tf_op jit(solution)/shard_map/psum | solution.py:82
  340.7 8.2 %add_reduce_fusion.4 = f32[8,8,8,64]{3,2,1,0:T(8,128)S(1)} fusion(f32[8,8,8,64,64]{3,4,2,1,0:T(8,128)} %get-tuple-element.107, f32[8,8,64]{2,1,0:T(8,128)S(1)} %add.166), kind=kLoop, calls=%fused_computation.38 | loop fusion | flops 4161536 | bytes 8536064 | tf_op jit(solution)/shard_map/reduce_max | solution.py:88
  348.9 11.1 %exponential_reduce_fusion.4 = f32[8,8,8,64]{3,2,1,0:T(8,128)S(1)} fusion(f32[8,8,8,64,64]{3,4,2,1,0:T(8,128)} %get-tuple-element.107, f32[8,8,8,64]{3,2,1,0:T(8,128)S(1)} %add_reduce_fusion.4, f32[8,8,64]{2,1,0:T(8,128)S(1)} %add.166), kind=kLoop, calls=%fused_computation.32 | loop fusion | flops 6258688 | bytes 8667136 | tf_op jit(solution)/shard_map/reduce_sum | solution.py:89
  359.9 6.7 while.44
  360.0 3.2 select_reduce_fusion.6
  363.3 3.2 select_reduce_fusion.6
  366.8 1.0 gather_fusion.2
  368.5 35.2 %pmax.43 = f32[8192]{0:T(1024)S(1)} all-reduce(f32[8192]{0:T(1024)S(1)} %reshape.249), channel_id=1, replica_groups=mesh['item'=8,'code'=4] {'item'}, use_global_device_ids=true, to_apply=%region_15.16 | all-reduce | flops 8192 | bytes 65536 | tf_op jit(solution)/shard_map/pmax | solution.py:119
  403.7 33.0 %psum.59 = f32[8192]{0:T(1024)S(1)} all-reduce(f32[8192]{0:T(1024)S(1)} %exponential_multiply_fusion.2), channel_id=1, replica_groups=mesh['item'=8,'code'=4] {'item'}, use_global_device_ids=true, to_apply=%region_17.18 | all-reduce | flops 8192 | bytes 65536 | tf_op jit(solution)/shard_map/psum | solution.py:120
  437.5 1.0 gather_fusion.3
  438.6 7.6 %add_reduce_fusion.3 = f32[8,8,64]{2,1,0:T(8,128)S(1)} fusion(f32[8,8,8,64,64]{3,4,2,1,0:T(8,128)} %get-tuple-element.107, f32[8,8,8,64]{3,2,1,0:T(8,128)S(1)} %bitcast.101), kind=kLoop, calls=%fused_computation.37 | loop fusion | flops 4190208 | bytes 8536064 | tf_op jit(solution)/shard_map/reduce_max | solution.py:74
  446.2 7.6 %exponential_reduce_fusion.3 = f32[8,8,64]{2,1,0:T(8,128)S(1)} fusion(f32[8,8,8,64,64]{3,4,2,1,0:T(8,128)} %get-tuple-element.107, f32[8,8,64]{2,1,0:T(8,128)S(1)} %add_reduce_fusion.3, f32[8,8,8,64]{3,2,1,0:T(8,128)S(1)} %bitcast.102), kind=kLoop, calls=%fused_computation.31 | loop fusion | flops 6287360 | bytes 8552448 | tf_op jit(solution)/shard_map/reduce_sum | solution.py:75
  454.0 10.1 %pmax.44 = f32[4096]{0:T(1024)S(1)} all-reduce(f32[4096]{0:T(1024)S(1)} %reshape.254), channel_id=1, replica_groups=mesh['item'=8,'code'=4] {'code'}, use_global_device_ids=true, to_apply=%region_19.20 | all-reduce | flops 4096 | bytes 32768 | tf_op jit(solution)/shard_map/pmax | solution.py:81
  464.1 10.1 %psum.60 = f32[4096]{0:T(1024)S(1)} all-reduce(f32[4096]{0:T(1024)S(1)} %exponential_multiply_fusion.4), channel_id=1, replica_groups=mesh['item'=8,'code'=4] {'code'}, use_global_device_ids=true, to_apply=%region_21.22 | all-reduce | flops 4096 | bytes 32768 | tf_op jit(solution)/shard_map/psum | solution.py:82
  474.3 8.2 %add_reduce_fusion.2 = f32[8,8,8,64]{3,2,1,0:T(8,128)S(1)} fusion(f32[8,8,8,64,64]{3,4,2,1,0:T(8,128)} %get-tuple-element.107, f32[8,8,64]{2,1,0:T(8,128)S(1)} %add.175), kind=kLoop, calls=%fused_computation.36 | loop fusion | flops 4161536 | bytes 8536064 | tf_op jit(solution)/shard_map/reduce_max | solution.py:88
  482.5 11.1 %exponential_reduce_fusion.2 = f32[8,8,8,64]{3,2,1,0:T(8,128)S(1)} fusion(f32[8,8,8,64,64]{3,4,2,1,0:T(8,128)} %get-tuple-element.107, f32[8,8,8,64]{3,2,1,0:T(8,128)S(1)} %add_reduce_fusion.2, f32[8,8,64]{2,1,0:T(8,128)S(1)} %add.175), kind=kLoop, calls=%fused_computation.30 | loop fusion | flops 6258688 | bytes 8667136 | tf_op jit(solution)/shard_map/reduce_sum | solution.py:89
  493.6 6.7 while.45
  493.6 3.2 select_reduce_fusion.7
  497.0 3.2 select_reduce_fusion.7
  500.4 1.0 gather_fusion.4
  502.1 33.0 %pmax.45 = f32[8192]{0:T(1024)S(1)} all-reduce(f32[8192]{0:T(1024)S(1)} %reshape.256), channel_id=1, replica_groups=mesh['item'=8,'code'=4] {'item'}, use_global_device_ids=true, to_apply=%region_26.27 | all-reduce | flops 8192 | bytes 65536 | tf_op jit(solution)/shard_map/pmax | solution.py:119
  535.2 33.2 %psum.61 = f32[8192]{0:T(1024)S(1)} all-reduce(f32[8192]{0:T(1024)S(1)} %exponential_multiply_fusion.1), channel_id=1, replica_groups=mesh['item'=8,'code'=4] {'item'}, use_global_device_ids=true, to_apply=%region_28.29 | all-reduce | flops 8192 | bytes 65536 | tf_op jit(solution)/shard_map/psum | solution.py:120
  568.5 1.0 gather_fusion.5
  569.5 7.6 %add_reduce_fusion.1 = f32[8,8,64]{2,1,0:T(8,128)S(1)} fusion(f32[8,8,8,64,64]{3,4,2,1,0:T(8,128)} %get-tuple-element.107, f32[8,8,8,64]{3,2,1,0:T(8,128)S(1)} %bitcast.99), kind=kLoop, calls=%fused_computation.35 | loop fusion | flops 4190208 | bytes 8536064 | tf_op jit(solution)/shard_map/reduce_max | solution.py:74
  577.1 7.6 %exponential_reduce_fusion.1 = f32[8,8,64]{2,1,0:T(8,128)S(1)} fusion(f32[8,8,8,64,64]{3,4,2,1,0:T(8,128)} %get-tuple-element.107, f32[8,8,64]{2,1,0:T(8,128)S(1)} %add_reduce_fusion.1, f32[8,8,8,64]{3,2,1,0:T(8,128)S(1)} %bitcast.100), kind=kLoop, calls=%fused_computation.29 | loop fusion | flops 6287360 | bytes 8552448 | tf_op jit(solution)/shard_map/reduce_sum | solution.py:75
  584.9 10.1 %pmax.46 = f32[4096]{0:T(1024)S(1)} all-reduce(f32[4096]{0:T(1024)S(1)} %reshape.261), channel_id=1, replica_groups=mesh['item'=8,'code'=4] {'code'}, use_global_device_ids=true, to_apply=%region_30.31 | all-reduce | flops 4096 | bytes 32768 | tf_op jit(solution)/shard_map/pmax | solution.py:81
  595.0 10.1 %psum.62 = f32[4096]{0:T(1024)S(1)} all-reduce(f32[4096]{0:T(1024)S(1)} %exponential_multiply_fusion.3), channel_id=1, replica_groups=mesh['item'=8,'code'=4] {'code'}, use_global_device_ids=true, to_apply=%region_32.33 | all-reduce | flops 4096 | bytes 32768 | tf_op jit(solution)/shard_map/psum | solution.py:82
  605.2 8.2 %add_reduce_fusion = f32[8,8,8,64]{3,2,1,0:T(8,128)S(1)} fusion(f32[8,8,8,64,64]{3,4,2,1,0:T(8,128)} %get-tuple-element.107, f32[8,8,64]{2,1,0:T(8,128)S(1)} %add.183), kind=kLoop, calls=%fused_computation.34 | loop fusion | flops 4161536 | bytes 8536064 | tf_op jit(solution)/shard_map/reduce_max | solution.py:88
  613.5 11.1 %exponential_reduce_fusion = f32[8,8,8,64]{3,2,1,0:T(8,128)S(1)} fusion(f32[8,8,8,64,64]{3,4,2,1,0:T(8,128)} %get-tuple-element.107, f32[8,8,8,64]{3,2,1,0:T(8,128)S(1)} %add_reduce_fusion, f32[8,8,64]{2,1,0:T(8,128)S(1)} %add.183), kind=kLoop, calls=%fused_computation.28 | loop fusion | flops 6258688 | bytes 8667136 | tf_op jit(solution)/shard_map/reduce_sum | solution.py:89
  624.5 6.7 while.46
  624.6 3.2 select_reduce_fusion.8
  627.9 3.2 select_reduce_fusion.8
  631.4 1.0 gather_fusion.6
  633.1 33.0 %pmax.47 = f32[8192]{0:T(1024)S(1)} all-reduce(f32[8192]{0:T(1024)S(1)} %reshape.263), channel_id=1, replica_groups=mesh['item'=8,'code'=4] {'item'}, use_global_device_ids=true, to_apply=%region_37.38 | all-reduce | flops 8192 | bytes 65536 | tf_op jit(solution)/shard_map/pmax | solution.py:119
  666.1 33.0 %psum.63 = f32[8192]{0:T(1024)S(1)} all-reduce(f32[8192]{0:T(1024)S(1)} %exponential_multiply_fusion), channel_id=1, replica_groups=mesh['item'=8,'code'=4] {'item'}, use_global_device_ids=true, to_apply=%region_39.40 | all-reduce | flops 8192 | bytes 65536 | tf_op jit(solution)/shard_map/psum | solution.py:120
  (166 shorter events, 16.8 us)
Async XLA Ops:
  7.2 28.2 %copy-start = (s32[64,16]{0,1:T(8,128)S(1)}, s32[64,16]{0,1:T(8,128)}, u32[]{:S(2)}) copy-start(s32[64,16]{0,1:T(8,128)} %param.17) | copy-start | bytes 12292
  7.2 39.6 %all-gather.5.cloned.1.call-start = ((), (), s32[]{:S(2)}) async-start(), calls=%async_computation.1 | async-start | bytes 5242880 | tf_op jit(solution)/shard_map/all_gather | solution.py:14
  7.9 165.5 %all-gather.3.cloned.1.call-start = ((), (), s32[]{:S(2)}) async-start(), calls=%async_computation | async-start | bytes 9437184 | tf_op jit(solution)/shard_map/all_gather | solution.py:15
  35.4 4.6 copy-start.2
  302.9 10.7 %copy-start.1 = (f32[8,8,8,64,64]{3,4,2,1,0:T(8,128)S(1)}, f32[8,8,8,64,64]{3,4,2,1,0:T(8,128)}, u32[]{:S(2)}) copy-start(f32[8,8,8,64,64]{3,4,2,1,0:T(8,128)} %get-tuple-element.107) | copy-start | bytes 25165828
  302.9 37.6 %copy-start.3 = (f32[4096]{0:T(1024)S(1)}, f32[4096]{0:T(1024)}, u32[]{:S(2)}) copy-start(f32[4096]{0:T(1024)} %param.15) | copy-start | bytes 49156
  605.2 19.4 %copy-start.4 = (f32[4096]{0:T(1024)}, f32[4096]{0:T(1024)S(1)}, u32[]{:S(2)}) copy-start(f32[4096]{0:T(1024)S(1)} %add_subtract_fusion.3) | copy-start | bytes 49156
Sparse Core Ops, SparseCore 0:
  9.5 37.1 all-gather.4
  48.9 124.4 all-gather.2
where the time goes:
time: 708 us; the launch traced here: 707 us
  blocking collectives  286 us (40%)
  waiting for transfers between devices  127 us (18%)
  other arithmetic  127 us (18%)
  local copies, waits for them, and re-layouts  85.9 us (12%)
  matrix products  59.6 us (8%)
  between operations  15.8 us (2%)
    all_gather x1, waiting for transfers between devices, body(): code_cols = lax.all_gather(codebook, 'item', axis=0, tiled=True)  121 us
    pmax x3, blocking collectives, body(): joined_peak = lax.pmax(col_peak, 'item')  101 us
    psum x3, blocking collectives, body(): joined_total = lax.psum(col_total * jnp.exp(col_peak - joined_peak), 'item')  99.3 us
    dot_general x8, matrix products, build_tiles(): jnp.einsum('rbi,rbsj->bsij', own, picked, precision=lax.Precision.HIGHEST)  58.1 us
    gather x8, local copies, waits for them, and re-layouts, build_tiles(): picked = code_column_splits[:, ids, :]  49.4 us
    reduce_sum x3, other arithmetic, col_reduce(): block_total = jnp.sum(jnp.exp(logits - block_peak[:, :, None, :]), axis=2)  33.2 us
    psum x3, blocking collectives, body(): merged_total = lax.psum(row_total * jnp.exp(row_peak - merged_peak), 'code')  31.6 us
    pmax x3, blocking collectives, body(): merged_peak = lax.pmax(row_peak, 'code')  30.4 us
  transfers between devices with their start and end apart: 2, of which 2 were waited for; matrix products, arithmetic and copies ran while one was open for 2% of the time, Pallas kernels for 0%

commit v1 on v0

--- a/solution.py
+++ b/solution.py
@@ -117,7 +117,9 @@
         col_peak = col_peak.reshape(code_count)
         col_total = col_total.reshape(code_count)
         joined_peak = lax.pmax(col_peak, "item")
-        joined_total = lax.psum(col_total * jnp.exp(col_peak - joined_peak), "item")
+        joined_total = jnp.sum(
+            lax.all_gather(col_total * jnp.exp(col_peak - joined_peak), "item"), axis=0
+        )
         code_potential = code_logmass - (joined_peak + jnp.log(joined_total))
     return (item_potential, code_potential)
 

time: 708 us -> 702 us (level)
    psum x3 -> x0, blocking collectives: 99.3 us -> none  [body(): joined_total = lax.psum(col_total * jnp.exp(col_peak - joined_peak), 'item')]
    all_gather x0 -> x3, blocking collectives: none -> 92.7 us  [body(): lax.all_gather(col_total * jnp.exp(col_peak - joined_peak), 'item')]
where the time goes in v1:
time: 702 us; the launch traced here: 700 us
  blocking collectives  280 us (40%)
  waiting for transfers between devices  127 us (18%)
  other arithmetic  127 us (18%)
  local copies, waits for them, and re-layouts  86.1 us (12%)
  matrix products  59.6 us (8%)
  between operations  15.8 us (2%)
    all_gather x1, waiting for transfers between devices, body(): code_cols = lax.all_gather(codebook, 'item', axis=0, tiled=True)  121 us
    pmax x3, blocking collectives, body(): joined_peak = lax.pmax(col_peak, 'item')  101 us
    all_gather x3, blocking collectives, body(): lax.all_gather(col_total * jnp.exp(col_peak - joined_peak), 'item')  92.7 us
    dot_general x8, matrix products, build_tiles(): jnp.einsum('rbi,rbsj->bsij', own, picked, precision=lax.Precision.HIGHEST)  58.1 us
    gather x8, local copies, waits for them, and re-layouts, build_tiles(): picked = code_column_splits[:, ids, :]  49.4 us
    reduce_sum x3, other arithmetic, col_reduce(): block_total = jnp.sum(jnp.exp(logits - block_peak[:, :, None, :]), axis=2)  33.2 us
    psum x3, blocking collectives, body(): merged_total = lax.psum(row_total * jnp.exp(row_peak - merged_peak), 'code')  31.6 us
    pmax x3, blocking collectives, body(): merged_peak = lax.pmax(row_peak, 'code')  30.4 us
  transfers between devices with their start and end apart: 2, of which 2 were waited for; matrix products, arithmetic and copies ran while one was open for 2% of the time, Pallas kernels for 0%

profile of v1, /device:TPU:0, one launch (start us, length us, event | category | flops | bytes accessed | tf_op | source)
XLA Modules:
  0.0 700.4 jit_solution(4799150685524247314)
XLA Ops:
  8.7 1.3 reduce_sum.99
  10.0 23.8 %psum.35 = f32[]{:T(128)} all-reduce(f32[]{:T(128)} %reduce_sum.99), channel_id=1, replica_groups=mesh['item'=8,'code'=4] {'item'}, use_global_device_ids=true, to_apply=%region_1.0 | all-reduce | flops 1 | bytes 8 | tf_op jit(solution)/shard_map/psum | solution.py:22
  35.4 3.9 gather_fusion.7
  41.4 1.0 gather_fusion.1
  42.6 4.1 all-gather.8.cloned.1.call-done
  46.8 5.6 copy.38
  52.4 121.0 %all-gather.6.cloned.1.call-done = f32[256,8192]{1,0:T(8,128)} async-done(((f32[32,8192]{1,0:T(8,128)}), f32[256,8192]{1,0:T(8,128)}) %all-gather.6.cloned.1.call-update) | async-done | bytes 8388624 | tf_op jit(solution)/shard_map/all_gather | solution.py:15
  173.4 9.0 %copy.37 = f32[256,8192]{0,1:T(8,128)} copy(f32[256,8192]{1,0:T(8,128)} %all-gather.6.cloned.1.call-done) | data formatting | bytes 16777216 | tf_op jit(solution)/shard_map/all_gather | solution.py:15
  182.4 120.6 %while.43 = (s32[]{:T(128)}, f32[8,8,8,64,64]{3,4,2,1,0:T(8,128)}, s32[8]{0:T(128)S(1)}, pred[64,8]{0,1:T(8,128)(4,1)S(1)}, s32[64,8]{0,1:T(8,128)S(1)}, /*index...) while((s32[]{:T(128)}, f32[8,8,8,64,64]{3,4,2,1,0:T(8,128)}, ...), condition=%wide.region_4.0_spmd, body=%wide.region_3.0_spmd.sunk | while | flops 805831872 | bytes 15212019 | solution.py:55
  183.9 6.2 gather_fusion
  190.2 7.3 %bitcast_dynamic-update-slice_fusion.2 = f32[8,8,8,64,64]{3,4,2,1,0:T(8,128)} fusion(f32[8,8,8,64,64]{3,4,2,1,0:T(8,128)} %get-tuple-element.349, s32[]{:T(128)} %get-tuple-element.348, f32[256,8,8,64]{0,3,2,1:T(8,128)} %bitcast.88, pred[8,8]{1,0:T(8,128)(4,1)S(1)} %copy.63, f32[256,64,64]{0,2,1:T(8,128)} %get-tuple-element.365, s32[]{:T(128)S(6)} %select_n.148), kind=kOutput, calls=%fused_computation.8.clone.1 | convolution fusion | flops 805830656 | bytes 6816324 | tf_op jit(solution)/shard_map/while/body/eval_jaxpr/rbi,rbsj->bsij/dot_general | solution.py:41
  199.0 6.2 gather_fusion
  205.3 7.2 %bitcast_dynamic-update-slice_fusion.2 = f32[8,8,8,64,64]{3,4,2,1,0:T(8,128)} fusion(f32[8,8,8,64,64]{3,4,2,1,0:T(8,128)} %get-tuple-element.349, s32[]{:T(128)} %get-tuple-element.348, f32[256,8,8,64]{0,3,2,1:T(8,128)} %bitcast.88, pred[8,8]{1,0:T(8,128)(4,1)S(1)} %copy.63, f32[256,64,64]{0,2,1:T(8,128)} %get-tuple-element.365, s32[]{:T(128)S(6)} %select_n.148), kind=kOutput, calls=%fused_computation.8.clone.1 | convolution fusion | flops 805830656 | bytes 6816324 | tf_op jit(solution)/shard_map/while/body/eval_jaxpr/rbi,rbsj->bsij/dot_general | solution.py:41
  214.0 6.2 gather_fusion
  220.3 7.3 %bitcast_dynamic-update-slice_fusion.2 = f32[8,8,8,64,64]{3,4,2,1,0:T(8,128)} fusion(f32[8,8,8,64,64]{3,4,2,1,0:T(8,128)} %get-tuple-element.349, s32[]{:T(128)} %get-tuple-element.348, f32[256,8,8,64]{0,3,2,1:T(8,128)} %bitcast.88, pred[8,8]{1,0:T(8,128)(4,1)S(1)} %copy.63, f32[256,64,64]{0,2,1:T(8,128)} %get-tuple-element.365, s32[]{:T(128)S(6)} %select_n.148), kind=kOutput, calls=%fused_computation.8.clone.1 | convolution fusion | flops 805830656 | bytes 6816324 | tf_op jit(solution)/shard_map/while/body/eval_jaxpr/rbi,rbsj->bsij/dot_general | solution.py:41
  229.0 6.2 gather_fusion
  235.4 7.3 %bitcast_dynamic-update-slice_fusion.2 = f32[8,8,8,64,64]{3,4,2,1,0:T(8,128)} fusion(f32[8,8,8,64,64]{3,4,2,1,0:T(8,128)} %get-tuple-element.349, s32[]{:T(128)} %get-tuple-element.348, f32[256,8,8,64]{0,3,2,1:T(8,128)} %bitcast.88, pred[8,8]{1,0:T(8,128)(4,1)S(1)} %copy.63, f32[256,64,64]{0,2,1:T(8,128)} %get-tuple-element.365, s32[]{:T(128)S(6)} %select_n.148), kind=kOutput, calls=%fused_computation.8.clone.1 | convolution fusion | flops 805830656 | bytes 6816324 | tf_op jit(solution)/shard_map/while/body/eval_jaxpr/rbi,rbsj->bsij/dot_general | solution.py:41
  244.1 6.2 gather_fusion
  250.4 7.3 %bitcast_dynamic-update-slice_fusion.2 = f32[8,8,8,64,64]{3,4,2,1,0:T(8,128)} fusion(f32[8,8,8,64,64]{3,4,2,1,0:T(8,128)} %get-tuple-element.349, s32[]{:T(128)} %get-tuple-element.348, f32[256,8,8,64]{0,3,2,1:T(8,128)} %bitcast.88, pred[8,8]{1,0:T(8,128)(4,1)S(1)} %copy.63, f32[256,64,64]{0,2,1:T(8,128)} %get-tuple-element.365, s32[]{:T(128)S(6)} %select_n.148), kind=kOutput, calls=%fused_computation.8.clone.1 | convolution fusion | flops 805830656 | bytes 6816324 | tf_op jit(solution)/shard_map/while/body/eval_jaxpr/rbi,rbsj->bsij/dot_general | solution.py:41
  259.2 6.2 gather_fusion
  265.6 7.2 %bitcast_dynamic-update-slice_fusion.2 = f32[8,8,8,64,64]{3,4,2,1,0:T(8,128)} fusion(f32[8,8,8,64,64]{3,4,2,1,0:T(8,128)} %get-tuple-element.349, s32[]{:T(128)} %get-tuple-element.348, f32[256,8,8,64]{0,3,2,1:T(8,128)} %bitcast.88, pred[8,8]{1,0:T(8,128)(4,1)S(1)} %copy.63, f32[256,64,64]{0,2,1:T(8,128)} %get-tuple-element.365, s32[]{:T(128)S(6)} %select_n.148), kind=kOutput, calls=%fused_computation.8.clone.1 | convolution fusion | flops 805830656 | bytes 6816324 | tf_op jit(solution)/shard_map/while/body/eval_jaxpr/rbi,rbsj->bsij/dot_general | solution.py:41
  274.3 6.2 gather_fusion
  280.6 7.3 %bitcast_dynamic-update-slice_fusion.2 = f32[8,8,8,64,64]{3,4,2,1,0:T(8,128)} fusion(f32[8,8,8,64,64]{3,4,2,1,0:T(8,128)} %get-tuple-element.349, s32[]{:T(128)} %get-tuple-element.348, f32[256,8,8,64]{0,3,2,1:T(8,128)} %bitcast.88, pred[8,8]{1,0:T(8,128)(4,1)S(1)} %copy.63, f32[256,64,64]{0,2,1:T(8,128)} %get-tuple-element.365, s32[]{:T(128)S(6)} %select_n.148), kind=kOutput, calls=%fused_computation.8.clone.1 | convolution fusion | flops 805830656 | bytes 6816324 | tf_op jit(solution)/shard_map/while/body/eval_jaxpr/rbi,rbsj->bsij/dot_general | solution.py:41
  289.4 6.2 gather_fusion
  295.7 7.3 %bitcast_dynamic-update-slice_fusion.2 = f32[8,8,8,64,64]{3,4,2,1,0:T(8,128)} fusion(f32[8,8,8,64,64]{3,4,2,1,0:T(8,128)} %get-tuple-element.349, s32[]{:T(128)} %get-tuple-element.348, f32[256,8,8,64]{0,3,2,1:T(8,128)} %bitcast.88, pred[8,8]{1,0:T(8,128)(4,1)S(1)} %copy.63, f32[256,64,64]{0,2,1:T(8,128)} %get-tuple-element.365, s32[]{:T(128)S(6)} %select_n.148), kind=kOutput, calls=%fused_computation.8.clone.1 | convolution fusion | flops 805830656 | bytes 6816324 | tf_op jit(solution)/shard_map/while/body/eval_jaxpr/rbi,rbsj->bsij/dot_general | solution.py:41
  302.9 9.4 %add_reduce_fusion.5 = f32[8,8,64]{2,1,0:T(8,128)S(1)} fusion(f32[8,8,8,64,64]{3,4,2,1,0:T(8,128)} %get-tuple-element.107, f32[8,8,8,64]{3,2,1,0:T(8,128)S(1)} %bitcast.97), kind=kLoop, calls=%fused_computation.39 | loop fusion | flops 4190208 | bytes 8536064 | tf_op jit(solution)/shard_map/reduce_max | solution.py:74
  312.3 1.3 copy-done.1
  313.7 5.1 exponential_reduce_fusion.5
  319.0 10.2 %pmax.42 = f32[4096]{0:T(1024)S(1)} all-reduce(f32[4096]{0:T(1024)S(1)} %reshape.247), channel_id=1, replica_groups=mesh['item'=8,'code'=4] {'code'}, use_global_device_ids=true, to_apply=%region_8.9 | all-reduce | flops 4096 | bytes 32768 | tf_op jit(solution)/shard_map/pmax | solution.py:81
  329.2 11.4 %all-reduce.3 = (f32[4096]{0:T(1024)S(1)}, f32[]{:T(128)}) all-reduce(f32[4096]{0:T(1024)S(1)} %exponential_multiply_fusion.5, f32[]{:T(128)} %reduce_sum.100), channel_id=1, replica_groups=mesh['item'=8,'code'=4] {'code'}, use_global_device_ids=true, to_apply=%region_10.11 | all-reduce | flops 4097 | bytes 32776 | tf_op jit(solution)/shard_map/psum | solution.py:82
  340.7 8.2 %add_reduce_fusion.4 = f32[8,8,8,64]{3,2,1,0:T(8,128)S(1)} fusion(f32[8,8,8,64,64]{3,4,2,1,0:T(8,128)} %get-tuple-element.107, f32[8,8,64]{2,1,0:T(8,128)S(1)} %add.160), kind=kLoop, calls=%fused_computation.38 | loop fusion | flops 4161536 | bytes 8536064 | tf_op jit(solution)/shard_map/reduce_max | solution.py:88
  348.9 11.1 %exponential_reduce_fusion.4 = f32[8,8,8,64]{3,2,1,0:T(8,128)S(1)} fusion(f32[8,8,8,64,64]{3,4,2,1,0:T(8,128)} %get-tuple-element.107, f32[8,8,8,64]{3,2,1,0:T(8,128)S(1)} %add_reduce_fusion.4, f32[8,8,64]{2,1,0:T(8,128)S(1)} %add.160), kind=kLoop, calls=%fused_computation.32 | loop fusion | flops 6258688 | bytes 8667136 | tf_op jit(solution)/shard_map/reduce_sum | solution.py:89
  359.9 6.7 while.44
  360.0 3.2 select_reduce_fusion.6
  363.3 3.2 select_reduce_fusion.6
  366.8 1.0 gather_fusion.2
  368.5 35.2 %pmax.43 = f32[8192]{0:T(1024)S(1)} all-reduce(f32[8192]{0:T(1024)S(1)} %reshape.249), channel_id=1, replica_groups=mesh['item'=8,'code'=4] {'item'}, use_global_device_ids=true, to_apply=%region_15.16 | all-reduce | flops 8192 | bytes 65536 | tf_op jit(solution)/shard_map/pmax | solution.py:119
  403.7 30.7 %all-gather = f32[65536]{0:T(1024)S(1)} all-gather(f32[8192]{0:T(1024)S(1)} %exponential_multiply_fusion.2), channel_id=2, replica_groups=mesh['item'=8,'code'=4] {'item'}, dimensions={0}, use_global_device_ids=true | all-gather | bytes 294912 | tf_op jit(solution)/shard_map/all_gather | solution.py:121
  435.4 1.0 gather_fusion.3
  436.4 7.6 %add_reduce_fusion.3 = f32[8,8,64]{2,1,0:T(8,128)S(1)} fusion(f32[8,8,8,64,64]{3,4,2,1,0:T(8,128)} %get-tuple-element.107, f32[8,8,8,64]{3,2,1,0:T(8,128)S(1)} %bitcast.101), kind=kLoop, calls=%fused_computation.37 | loop fusion | flops 4190208 | bytes 8536064 | tf_op jit(solution)/shard_map/reduce_max | solution.py:74
  444.0 7.6 %exponential_reduce_fusion.3 = f32[8,8,64]{2,1,0:T(8,128)S(1)} fusion(f32[8,8,8,64,64]{3,4,2,1,0:T(8,128)} %get-tuple-element.107, f32[8,8,64]{2,1,0:T(8,128)S(1)} %add_reduce_fusion.3, f32[8,8,8,64]{3,2,1,0:T(8,128)S(1)} %bitcast.102), kind=kLoop, calls=%fused_computation.31 | loop fusion | flops 6287360 | bytes 8552448 | tf_op jit(solution)/shard_map/reduce_sum | solution.py:75
  451.8 10.1 %pmax.44 = f32[4096]{0:T(1024)S(1)} all-reduce(f32[4096]{0:T(1024)S(1)} %reshape.254), channel_id=1, replica_groups=mesh['item'=8,'code'=4] {'code'}, use_global_device_ids=true, to_apply=%region_19.20 | all-reduce | flops 4096 | bytes 32768 | tf_op jit(solution)/shard_map/pmax | solution.py:81
  461.9 10.1 %psum.38 = f32[4096]{0:T(1024)S(1)} all-reduce(f32[4096]{0:T(1024)S(1)} %exponential_multiply_fusion.4), channel_id=1, replica_groups=mesh['item'=8,'code'=4] {'code'}, use_global_device_ids=true, to_apply=%region_21.22 | all-reduce | flops 4096 | bytes 32768 | tf_op jit(solution)/shard_map/psum | solution.py:82
  472.1 8.2 %add_reduce_fusion.2 = f32[8,8,8,64]{3,2,1,0:T(8,128)S(1)} fusion(f32[8,8,8,64,64]{3,4,2,1,0:T(8,128)} %get-tuple-element.107, f32[8,8,64]{2,1,0:T(8,128)S(1)} %add.169), kind=kLoop, calls=%fused_computation.36 | loop fusion | flops 4161536 | bytes 8536064 | tf_op jit(solution)/shard_map/reduce_max | solution.py:88
  480.4 11.1 %exponential_reduce_fusion.2 = f32[8,8,8,64]{3,2,1,0:T(8,128)S(1)} fusion(f32[8,8,8,64,64]{3,4,2,1,0:T(8,128)} %get-tuple-element.107, f32[8,8,8,64]{3,2,1,0:T(8,128)S(1)} %add_reduce_fusion.2, f32[8,8,64]{2,1,0:T(8,128)S(1)} %add.169), kind=kLoop, calls=%fused_computation.30 | loop fusion | flops 6258688 | bytes 8667136 | tf_op jit(solution)/shard_map/reduce_sum | solution.py:89
  491.4 6.7 while.45
  491.5 3.2 select_reduce_fusion.7
  494.8 3.2 select_reduce_fusion.7
  498.3 1.0 gather_fusion.4
  500.0 33.0 %pmax.45 = f32[8192]{0:T(1024)S(1)} all-reduce(f32[8192]{0:T(1024)S(1)} %reshape.256), channel_id=1, replica_groups=mesh['item'=8,'code'=4] {'item'}, use_global_device_ids=true, to_apply=%region_26.27 | all-reduce | flops 8192 | bytes 65536 | tf_op jit(solution)/shard_map/pmax | solution.py:119
  533.0 31.1 %all-gather.1 = f32[65536]{0:T(1024)S(1)} all-gather(f32[8192]{0:T(1024)S(1)} %exponential_multiply_fusion.1), channel_id=3, replica_groups=mesh['item'=8,'code'=4] {'item'}, dimensions={0}, use_global_device_ids=true | all-gather | bytes 294912 | tf_op jit(solution)/shard_map/all_gather | solution.py:121
  564.3 1.0 gather_fusion.5
  565.3 7.6 %add_reduce_fusion.1 = f32[8,8,64]{2,1,0:T(8,128)S(1)} fusion(f32[8,8,8,64,64]{3,4,2,1,0:T(8,128)} %get-tuple-element.107, f32[8,8,8,64]{3,2,1,0:T(8,128)S(1)} %bitcast.99), kind=kLoop, calls=%fused_computation.35 | loop fusion | flops 4190208 | bytes 8536064 | tf_op jit(solution)/shard_map/reduce_max | solution.py:74
  572.9 7.6 %exponential_reduce_fusion.1 = f32[8,8,64]{2,1,0:T(8,128)S(1)} fusion(f32[8,8,8,64,64]{3,4,2,1,0:T(8,128)} %get-tuple-element.107, f32[8,8,64]{2,1,0:T(8,128)S(1)} %add_reduce_fusion.1, f32[8,8,8,64]{3,2,1,0:T(8,128)S(1)} %bitcast.100), kind=kLoop, calls=%fused_computation.29 | loop fusion | flops 6287360 | bytes 8552448 | tf_op jit(solution)/shard_map/reduce_sum | solution.py:75
  580.7 10.1 %pmax.46 = f32[4096]{0:T(1024)S(1)} all-reduce(f32[4096]{0:T(1024)S(1)} %reshape.261), channel_id=1, replica_groups=mesh['item'=8,'code'=4] {'code'}, use_global_device_ids=true, to_apply=%region_30.31 | all-reduce | flops 4096 | bytes 32768 | tf_op jit(solution)/shard_map/pmax | solution.py:81
  590.8 10.1 %psum.39 = f32[4096]{0:T(1024)S(1)} all-reduce(f32[4096]{0:T(1024)S(1)} %exponential_multiply_fusion.3), channel_id=1, replica_groups=mesh['item'=8,'code'=4] {'code'}, use_global_device_ids=true, to_apply=%region_32.33 | all-reduce | flops 4096 | bytes 32768 | tf_op jit(solution)/shard_map/psum | solution.py:82
  601.1 8.2 %add_reduce_fusion = f32[8,8,8,64]{3,2,1,0:T(8,128)S(1)} fusion(f32[8,8,8,64,64]{3,4,2,1,0:T(8,128)} %get-tuple-element.107, f32[8,8,64]{2,1,0:T(8,128)S(1)} %add.177), kind=kLoop, calls=%fused_computation.34 | loop fusion | flops 4161536 | bytes 8536064 | tf_op jit(solution)/shard_map/reduce_max | solution.py:88
  609.3 11.1 %exponential_reduce_fusion = f32[8,8,8,64]{3,2,1,0:T(8,128)S(1)} fusion(f32[8,8,8,64,64]{3,4,2,1,0:T(8,128)} %get-tuple-element.107, f32[8,8,8,64]{3,2,1,0:T(8,128)S(1)} %add_reduce_fusion, f32[8,8,64]{2,1,0:T(8,128)S(1)} %add.177), kind=kLoop, calls=%fused_computation.28 | loop fusion | flops 6258688 | bytes 8667136 | tf_op jit(solution)/shard_map/reduce_sum | solution.py:89
  620.4 6.7 while.46
  620.4 3.2 select_reduce_fusion.8
  623.7 3.2 select_reduce_fusion.8
  627.2 1.0 gather_fusion.6
  628.9 33.0 %pmax.47 = f32[8192]{0:T(1024)S(1)} all-reduce(f32[8192]{0:T(1024)S(1)} %reshape.263), channel_id=1, replica_groups=mesh['item'=8,'code'=4] {'item'}, use_global_device_ids=true, to_apply=%region_37.38 | all-reduce | flops 8192 | bytes 65536 | tf_op jit(solution)/shard_map/pmax | solution.py:119
  661.9 30.9 %all-gather.2 = f32[65536]{0:T(1024)S(1)} all-gather(f32[8192]{0:T(1024)S(1)} %exponential_multiply_fusion), channel_id=4, replica_groups=mesh['item'=8,'code'=4] {'item'}, dimensions={0}, use_global_device_ids=true | all-gather | bytes 294912 | tf_op jit(solution)/shard_map/all_gather | solution.py:121
  (172 shorter events, 17.2 us)
Async XLA Ops:
  7.2 28.2 %copy-start = (s32[64,16]{0,1:T(8,128)S(1)}, s32[64,16]{0,1:T(8,128)}, u32[]{:S(2)}) copy-start(s32[64,16]{0,1:T(8,128)} %param.17) | copy-start | bytes 12292
  7.2 39.6 %all-gather.8.cloned.1.call-start = ((), (), s32[]{:S(2)}) async-start(), calls=%async_computation.1 | async-start | bytes 5242880 | tf_op jit(solution)/shard_map/all_gather | solution.py:14
  7.9 165.5 %all-gather.6.cloned.1.call-start = ((), (), s32[]{:S(2)}) async-start(), calls=%async_computation | async-start | bytes 9437184 | tf_op jit(solution)/shard_map/all_gather | solution.py:15
  35.4 4.6 copy-start.2
  302.9 10.7 %copy-start.1 = (f32[8,8,8,64,64]{3,4,2,1,0:T(8,128)S(1)}, f32[8,8,8,64,64]{3,4,2,1,0:T(8,128)}, u32[]{:S(2)}) copy-start(f32[8,8,8,64,64]{3,4,2,1,0:T(8,128)} %get-tuple-element.107) | copy-start | bytes 25165828
  302.9 37.6 %copy-start.3 = (f32[4096]{0:T(1024)S(1)}, f32[4096]{0:T(1024)}, u32[]{:S(2)}) copy-start(f32[4096]{0:T(1024)} %param.15) | copy-start | bytes 49156
  601.0 19.4 %copy-start.4 = (f32[4096]{0:T(1024)}, f32[4096]{0:T(1024)S(1)}, u32[]{:S(2)}) copy-start(f32[4096]{0:T(1024)S(1)} %add_subtract_fusion.3) | copy-start | bytes 49156
Sparse Core Ops, SparseCore 0:
  9.5 37.1 all-gather.7
  48.9 124.4 all-gather.5
